TPU v7x, 768 devices: a whole 4x8x12 slice. The times are simulated.
768 devices in a mesh: rep: 96 (over z_hi, x, y), fsdp: 8 (over z_lo, core).
Axes of the slice: x: 4, y: 8, z: 12 (z_hi: 3, z_lo: 4; z = z_hi * 4 + z_lo), core: 2. Of those that a mesh axis runs over, the one named last changes fastest.
Arguments:
- tokens: bfloat16 [98304, 4096], P(('rep', 'fsdp')), may hold values from -6 to 6
- queries: bfloat16 [98304, 2048], P(('rep', 'fsdp')), may hold values from -10 to 10
- rotated_key_rows: bfloat16 [98304, 512], P(('rep', 'fsdp')), may hold values from -3 to 3
- targets: bfloat16 [98304, 2048], P(('rep', 'fsdp')), may hold values from -6 to 6
- value_weights: float32 [4096, 512], P('fsdp'), may hold values from -4 to 4
- momentum: float32 [4096, 512], P('fsdp'), may hold values from -0.6 to 0.6
- first_moment: float32 [96, 4096, 512], P('rep', 'fsdp'), may hold values from -1.8 to 1.8
- second_moment: float32 [96, 4096, 512], P('rep', 'fsdp'), may hold values from 0.02 to 0.5
Outputs:
- new_weights: float32 [4096, 512], P('fsdp')
- new_momentum: float32 [4096, 512], P('fsdp')
All inputs are finite; a program needn't handle non-finite values.
Results may differ from a plain program's by a relative error of at most 0.0045.
Values may be sent and summed in bfloat16 or wider, within the bound.
A program may use at most 64 MiB of HBM per device.

v0:
```python
import math

import jax
import jax.numpy as jnp
from jax import lax
from jax.sharding import PartitionSpec as P

D = 4096
HEAD_SIZE = 128


first_decay = 0.9
second_decay = 0.95
weight_decay = 0.1
inner_rate = 0.05
outer_rate = 0.7
momentum_keep = 0.9
epsilon = 1e-08


def per_device(
    tokens, queries, rotated_key_rows, targets, value_weights, momentum, first_moment, second_moment
):
    kv_width = value_weights.shape[1]
    seq_len = tokens.shape[0]
    groups = rotated_key_rows.shape[1] // HEAD_SIZE
    heads_per_group = queries.shape[1] // rotated_key_rows.shape[1]
    replica_tokens = seq_len * lax.axis_size("fsdp")
    inv_root = 1.0 / math.sqrt(D)
    score_scale = 1.0 / math.sqrt(HEAD_SIZE)
    cot_scale = math.sqrt(D / replica_tokens)
    compact = value_weights.astype(jnp.bfloat16)
    feature_cols = tokens
    value_sum = jnp.dot(
        feature_cols,
        lax.all_gather(compact, "fsdp", axis=0, tiled=True),
        preferred_element_type=jnp.float32,
    )
    value_result = (value_sum * inv_root).astype(jnp.bfloat16)
    query_head_count = queries.reshape(seq_len, groups, heads_per_group, HEAD_SIZE)
    key_head_count = rotated_key_rows.reshape(seq_len, groups, HEAD_SIZE)
    value_head_count = value_result.reshape(seq_len, groups, HEAD_SIZE)
    scores = (
        jnp.einsum(
            "tgjd,sgd->gjts", query_head_count, key_head_count, preferred_element_type=jnp.float32
        )
        * score_scale
    )
    causal = lax.broadcasted_iota(jnp.int32, (seq_len, seq_len), 0) >= lax.broadcasted_iota(
        jnp.int32, (seq_len, seq_len), 1
    )
    scores = jnp.where(causal, scores, -jnp.inf)
    row_top = jnp.max(scores, axis=-1, keepdims=True)
    expo = jnp.exp(scores - row_top)
    probs = (expo / jnp.sum(expo, axis=-1, keepdims=True)).astype(jnp.bfloat16)
    outputs = jnp.einsum(
        "gjts,sgd->tgjd", probs, value_head_count, preferred_element_type=jnp.float32
    )
    objective = targets.reshape(seq_len, groups, heads_per_group, HEAD_SIZE).astype(jnp.float32)
    residual_term = ((outputs - objective) * cot_scale).astype(jnp.bfloat16)
    value_grad = jnp.einsum(
        "gjts,tgjd->sgd", probs, residual_term, preferred_element_type=jnp.float32
    )
    value_grad = value_grad.astype(jnp.bfloat16).reshape(seq_len, kv_width)
    feature_cols = tokens
    gradient = lax.psum_scatter(
        jnp.einsum(
            "si,sc->ic", feature_cols, value_grad, preferred_element_type=jnp.float32
        ).astype(jnp.bfloat16),
        "fsdp",
        scatter_dimension=0,
        tiled=True,
    ).astype(jnp.float32)
    gradient = gradient * inv_root
    first_new = first_decay * first_moment[0] + (1.0 - first_decay) * gradient
    second_new = second_decay * second_moment[0] + (1.0 - second_decay) * gradient * gradient
    direction = first_new / (jnp.sqrt(second_new) + epsilon) + weight_decay * value_weights
    mean_direction = lax.psum(direction, "rep") / lax.axis_size("rep")
    new_momentum = momentum_keep * momentum + mean_direction
    new_weights = value_weights - outer_rate * inner_rate * (
        mean_direction + momentum_keep * new_momentum
    )
    return (new_weights, new_momentum)


def solution(mesh):
    in_specs = (
        P(("rep", "fsdp"), None),
        P(("rep", "fsdp"), None),
        P(("rep", "fsdp"), None),
        P(("rep", "fsdp"), None),
        P("fsdp", None),
        P("fsdp", None),
        P("rep", "fsdp", None),
        P("rep", "fsdp", None),
    )
    out_specs = (P("fsdp", None), P("fsdp", None))
    return jax.shard_map(
        per_device, mesh=mesh, in_specs=in_specs, out_specs=out_specs, check_vma=False
    )
```

profile of v0, /device:TPU:62, one launch (start us, length us, event | category | flops | bytes accessed | tf_op | source)
XLA Modules:
  0.0 1371.9 jit_solution(4940539622195483337)
XLA Ops:
  7.2 0.0 copy-start
  7.2 0.0 copy-start.2
  7.2 0.0 all-gather.2.cloned.1.call-start
  7.2 2.2 convert_element_type.33
  9.4 0.0 all-gather.2.cloned.1.call-update
  9.4 0.0 reduce-scatter.2.cloned.1.call-start
  9.5 1.2 copy.28
  10.7 1.4 reshape.27
  12.1 0.0 copy-done.2
  12.2 1.4 fusion.37
  13.7 63.9 %all-gather.2.cloned.1.call-done = bf16[4096,512]{1,0:T(8,128)(2,1)} async-done(((bf16[512,512]{1,0:T(8,128)(2,1)}), bf16[4096,512]{1,0:T(8,128)(2,1)}) %all-gather.2.cloned.1.call-update) | async-done | bytes 4194320 | tf_op jit(solution)/shard_map/all_gather | solution.py:36
  77.5 0.0 copy-done
  77.5 2.9 fusion.12
  80.5 0.1 copy.25
  80.6 2.0 fusion.11
  82.6 0.0 copy-start.1
  82.6 3.2 fusion.1
  85.8 0.0 reduce-scatter.2.cloned.1.call-update
  85.8 0.0 all-reduce.2.cloned.1.call-start
  85.9 0.0 copy-done.1
  85.9 0.3 copy.18
  86.2 1.6 copy.15
  87.8 2.5 copy.10
  90.3 55.4 %reduce-scatter.2.cloned.1.call-done = bf16[512,512]{0,1:T(8,128)(2,1)} async-done(((bf16[4096,512]{0,1:T(8,128)(2,1)}), bf16[512,512]{0,1:T(8,128)(2,1)}) %reduce-scatter.2.cloned.1.call-update) | async-done | bytes 524304 | tf_op jit(solution)/shard_map/reduce_scatter | solution.py:66
  145.7 3.1 fusion.15
  148.8 0.0 all-reduce.2.cloned.1.call-update
  148.8 1.6 copy.17
  150.3 1207.1 %all-reduce.2.cloned.1.call-done = f32[512,512]{0,1:T(8,128)} async-done(((f32[512,512]{0,1:T(8,128)}), f32[512,512]{0,1:T(8,128)}) %all-reduce.2.cloned.1.call-update) | async-done | bytes 1048592 | tf_op jit(solution)/shard_map/psum | solution.py:78
  1357.4 2.9 multiply_add_fusion
  1360.3 2.5 copy.19
  1362.9 2.5 copy.20
  (2 shorter events, 0.1 us)
Async XLA Ops:
  7.2 70.4 %copy-start = (bf16[128,4096]{1,0:T(8,128)(2,1)S(1)}, bf16[128,4096]{1,0:T(8,128)(2,1)}, u32[]{:S(2)}) copy-start(bf16[128,4096]{1,0:T(8,128)(2,1)} %param.8) | copy-start | bytes 3145732
  7.2 5.0 copy-start.2
  7.2 70.4 %all-gather.2.cloned.1.call-start = ((), (), s32[]{:S(2)}) async-start(), calls=%async_computation.1 | async-start | bytes 4718592 | tf_op jit(solution)/shard_map/all_gather | solution.py:36
  9.4 136.2 %reduce-scatter.2.cloned.1.call-start = ((), (), s32[]{:S(2)}) async-start(), calls=%async_computation.2 | async-start | bytes 4718592 | tf_op jit(solution)/shard_map/reduce_scatter | solution.py:66
  82.6 3.3 copy-start.1
  85.8 1271.6 %all-reduce.2.cloned.1.call-start = ((), (), s32[]{:S(2)}) async-start(), calls=%async_computation.3 | async-start | bytes 2097152 | tf_op jit(solution)/shard_map/psum | solution.py:78
Sparse Core Ops, SparseCore 0:
  11.0 66.5 all-gather.1
  85.9 59.6 reduce-scatter.1
  149.5 1207.8 all-reduce.1
where the time goes:
time: 1370 us
  waiting for transfers between devices  1330 us (97%)
  local copies, waits for them, and re-layouts  13.9 us (1%)
  between operations  13.8 us (1%)
    psum x1, waiting for transfers between devices, per_device(): mean_direction = lax.psum(direction, 'rep') / lax.axis_size('rep')  1210 us
    all_gather x1, waiting for transfers between devices, per_device(): lax.all_gather(compact, 'fsdp', axis=0, tiled=True)  63.9 us
    reduce_scatter x1, waiting for transfers between devices, per_device(): lax.psum_scatter(jnp.einsum('si,sc->ic', feature_cols, value_grad, prefer...  55.4 us
  transfers between devices with their start and end apart: 3, of which 3 were waited for; matrix products, arithmetic and copies ran while one was open for 1% of the time, Pallas kernels for 0%

commit v1 on v0

v1 whole, which is shorter than its diff:
```python
import math

import jax
import jax.numpy as jnp
from jax import lax
from jax.experimental import pallas as pl
from jax.experimental.pallas import tpu as pltpu
from jax.sharding import PartitionSpec as P

D = 4096
HEAD = 128
NX, NY, NZH, NZL = 4, 8, 3, 4
NREP = NX * NY * NZH
NF = 8
SEQ = 128
KVW = 512
ROWS = 512
GROUPS = 4
HPG = 4
XR = ROWS // NX
YR = XR // NY
MESH = pl.DeviceIdType.MESH
BF = jnp.bfloat16
F32 = jnp.float32

first_decay = 0.9
second_decay = 0.95
weight_decay = 0.1
inner_rate = 0.05
outer_rate = 0.7
momentum_keep = 0.9
epsilon = 1e-08


def rows(start, size):
    return pl.ds(pl.multiple_of(start, size), size)


def kernel(
    tok_h, q_h, k_h, t_h, w_h, m1_h, m2_h, out_ref,
    tok, q, k, t, w, m1, m2,
    wall, tokc, vgall, probs, acc, dirs, xsend, xrecv, xsum, ysend, yrecv, zbuf, mean,
    loc, ws, wr, ts, tr, vs, vr, xs, xr, ys, yr, zs, zr, gs, gr, hs, hr,
):
    r = lax.axis_index("rep")
    f = lax.axis_index("fsdp")
    zh = lax.div(r, NX * NY)
    x = lax.rem(lax.div(r, NY), NX)
    y = lax.rem(r, NY)
    zl = lax.div(f, 2)
    c = lax.rem(f, 2)

    def dev(zh_=zh, x_=x, y_=y, f_=f):
        return {"rep": zh_ * (NX * NY) + x_ * NY + y_, "fsdp": f_}

    sib = f + 1 - 2 * c
    zl_r = lax.rem(zl + 1, NZL)
    zl_l = lax.rem(zl + NZL - 1, NZL)
    zl_o = lax.rem(zl + 2, NZL)
    zpos = zh * NZL + zl
    zp_r = lax.rem(zpos + 1, NZH * NZL)
    zp_l = lax.rem(zpos + NZH * NZL - 1, NZH * NZL)
    right = dev(zh_=lax.div(zp_r, NZL), f_=zl_r * 2 + c)
    left = dev(zh_=lax.div(zp_l, NZL), f_=zl_l * 2 + c)
    sibling = dev(f_=sib)

    loads = []
    for i, (src, dst) in enumerate(
        [(w_h, w), (tok_h, tok), (q_h, q), (k_h, k), (t_h, t), (m1_h, m1), (m2_h, m2)]
    ):
        cp = pltpu.make_async_copy(src, dst, loc.at[i])
        cp.start()
        loads.append(cp)

    barrier = pltpu.get_barrier_semaphore()
    peers = [right, left]
    peers += [dev(f_=lax.rem(f + d, NF)) for d in range(1, NF)]
    peers += [dev(x_=lax.rem(x + d, NX)) for d in range(1, NX)]
    peers += [dev(y_=lax.rem(y + d, NY)) for d in range(1, NY)]
    peers += [dev(zh_=lax.rem(zh + d, NZH)) for d in range(1, NZH)]
    for p in peers:
        pl.semaphore_signal(barrier, inc=1, device_id=p, device_id_type=MESH)

    loads[0].wait()
    wall[f] = w[...].astype(BF)
    pl.semaphore_wait(barrier, len(peers))

    def remote(src, dst, ss, rs, to):
        return pltpu.make_async_remote_copy(
            src_ref=src, dst_ref=dst, send_sem=ss, recv_sem=rs, device_id=to, device_id_type=MESH
        )

    H = ROWS // 2

    def whalf(slot, h):
        return wall.at[slot, pl.ds(h * H, H)]

    sends = []

    def go(cp):
        cp.start()
        sends.append(cp)

    go(remote(whalf(f, 0), whalf(f, 0), ws.at[0], wr.at[0], right))
    go(remote(whalf(f, 1), whalf(f, 1), ws.at[1], wr.at[1], left))
    go(remote(whalf(f, 1), whalf(f, 1), ws.at[2], wr.at[2], right))
    go(remote(whalf(f, 0), whalf(f, 0), ws.at[3], wr.at[3], left))
    go(remote(wall.at[f], wall.at[f], ws.at[4], wr.at[4], sibling))

    f_l = zl_l * 2 + c
    f_r = zl_r * 2 + c
    f_o = zl_o * 2 + c

    loads[2].wait()
    loads[3].wait()
    causal = lax.broadcasted_iota(jnp.int32, (SEQ, SEQ), 0) >= lax.broadcasted_iota(
        jnp.int32, (SEQ, SEQ), 1
    )
    score_scale = 1.0 / math.sqrt(HEAD)

    def scores_of(g):
        kg = k[:, g * HEAD : (g + 1) * HEAD]
        for j in range(HPG):
            h = g * HPG + j
            s = lax.dot_general(
                q[:, h * HEAD : (h + 1) * HEAD], kg, (((1,), (1,)), ((), ())),
                preferred_element_type=F32,
            )
            s = jnp.where(causal, s * score_scale, -jnp.inf)
            e = jnp.exp(s - jnp.max(s, axis=-1, keepdims=True))
            p = e / jnp.sum(e, axis=-1, keepdims=True)
            probs[g, j * SEQ : (j + 1) * SEQ, :] = p.astype(BF)

    loads[1].wait()

    def term(slot):
        return jnp.dot(
            tok[:, rows(slot * ROWS, ROWS)], wall[slot], preferred_element_type=F32
        )

    acc[...] = term(f)
    for g in range(GROUPS):
        scores_of(g)

    def got(buf, rs):
        remote(buf, buf, ws.at[0], rs, sibling).wait_recv()

    got(wall.at[sib], wr.at[4])
    acc[...] += term(sib)

    got(whalf(f_l, 0), wr.at[0])
    go(remote(whalf(f_l, 0), whalf(f_l, 0), ws.at[5], wr.at[5], right))
    got(whalf(f_r, 1), wr.at[1])
    go(remote(whalf(f_r, 1), whalf(f_r, 1), ws.at[6], wr.at[6], left))
    got(whalf(f_l, 1), wr.at[2])
    go(remote(wall.at[f_l], wall.at[f_l], ws.at[7], wr.at[7], sibling))
    got(whalf(f_r, 0), wr.at[3])
    go(remote(wall.at[f_r], wall.at[f_r], ws.at[8], wr.at[8], sibling))

    tsends = []
    order = [1, 2, 3]
    for n, dz in enumerate(order):
        for cc in range(2):
            to = lax.rem(zl + dz, NZL) * 2 + lax.rem(c + cc, 2)
            i = n * 2 + cc
            cp = remote(
                tok.at[:, rows(to * ROWS, ROWS)], tokc.at[rows(f * SEQ, SEQ)],
                ts.at[i], tr.at[i], dev(f_=to),
            )
            cp.start()
            tsends.append(cp)
    cp = remote(
        tok.at[:, rows(sib * ROWS, ROWS)], tokc.at[rows(f * SEQ, SEQ)], ts.at[6], tr.at[6], sibling
    )
    cp.start()
    tsends.append(cp)
    tokc[rows(f * SEQ, SEQ), :] = tok[:, rows(f * ROWS, ROWS)]

    acc[...] += term(f_l)
    acc[...] += term(f_r)
    got(wall.at[zl_l * 2 + 1 - c], wr.at[7])
    acc[...] += term(zl_l * 2 + 1 - c)
    got(wall.at[zl_r * 2 + 1 - c], wr.at[8])
    acc[...] += term(zl_r * 2 + 1 - c)
    got(whalf(f_o, 0), wr.at[5])
    go(remote(whalf(f_o, 0), whalf(f_o, 0), ws.at[9], wr.at[9], sibling))
    got(whalf(f_o, 1), wr.at[6])
    go(remote(whalf(f_o, 1), whalf(f_o, 1), ws.at[10], wr.at[10], sibling))
    acc[...] += term(f_o)
    f_os = zl_o * 2 + 1 - c
    got(whalf(f_os, 0), wr.at[9])
    got(whalf(f_os, 1), wr.at[10])
    acc[...] += term(f_os)

    inv_root = 1.0 / math.sqrt(D)
    cot_scale = math.sqrt(D / (SEQ * NF))
    loads[4].wait()
    for g in range(GROUPS):
        cols = slice(g * HEAD, (g + 1) * HEAD)
        v = (acc[:, cols] * inv_root).astype(BF)
        o = jnp.dot(probs[g], v, preferred_element_type=F32)
        tg = jnp.concatenate(
            [t[:, (g * HPG + j) * HEAD : (g * HPG + j + 1) * HEAD] for j in range(HPG)], axis=0
        )
        res = ((o - tg.astype(F32)) * cot_scale).astype(BF)
        vg = lax.dot_general(probs[g], res, (((0,), (0,)), ((), ())), preferred_element_type=F32)
        vgall[rows(f * SEQ, SEQ), cols] = vg.astype(BF)

    def vslot(s):
        return vgall.at[rows(s * SEQ, SEQ)]

    def vcopy(slot, i, to):
        return remote(vslot(slot), vslot(slot), vs.at[i], vr.at[i], to)

    right_f = dev(f_=jnp.minimum(f + 2, NF - 2 + c))
    left_f = dev(f_=jnp.maximum(f - 2, c))
    vcopy(f, 6, sibling).start()

    @pl.when(zl < NZL - 1)
    def _():
        vcopy(f, 0, right_f).start()

    @pl.when(zl > 0)
    def _():
        vcopy(f, 3, left_f).start()

    for h in range(1, NZL):
        @pl.when(zl >= h)
        def _():
            slot = f - 2 * h
            vcopy(slot, h - 1, sibling).wait_recv()
            if h < NZL - 1:
                @pl.when(zl < NZL - 1)
                def _():
                    vcopy(slot, h, right_f).start()
            vcopy(slot, 6 + h, sibling).start()

        @pl.when(zl + h < NZL)
        def _():
            slot = f + 2 * h
            vcopy(slot, 3 + h - 1, sibling).wait_recv()
            if h < NZL - 1:
                @pl.when(zl > 0)
                def _():
                    vcopy(slot, 3 + h, left_f).start()
            vcopy(slot, 9 + h, sibling).start()

    vcopy(sib, 6, sibling).wait_recv()
    for h in range(1, NZL):
        @pl.when(zl >= h)
        def _():
            vcopy(sib - 2 * h, 6 + h, sibling).wait_recv()

        @pl.when(zl + h < NZL)
        def _():
            vcopy(sib + 2 * h, 9 + h, sibling).wait_recv()

    for n, dz in enumerate(order):
        for cc in range(2):
            frm = lax.rem(zl + NZL - dz, NZL) * 2 + lax.rem(c + cc, 2)
            i = n * 2 + cc
            remote(
                tokc.at[rows(frm * SEQ, SEQ)], tokc.at[rows(frm * SEQ, SEQ)],
                ts.at[i], tr.at[i], sibling,
            ).wait_recv()
    remote(
        tokc.at[rows(sib * SEQ, SEQ)], tokc.at[rows(sib * SEQ, SEQ)], ts.at[6], tr.at[6], sibling
    ).wait_recv()

    loads[5].wait()
    loads[6].wait()

    def direction(q_):
        at = rows(q_ * XR, XR)
        grad = lax.dot_general(
            tokc[:, at], vgall[...], (((0,), (0,)), ((), ())), preferred_element_type=F32
        ) * inv_root
        fn = first_decay * m1[at, :] + (1.0 - first_decay) * grad
        sn = second_decay * m2[at, :] + (1.0 - second_decay) * grad * grad
        return fn / (jnp.sqrt(sn) + epsilon)

    xorder = [2, 1, 3]
    xsends = []
    for d in xorder:
        px = lax.rem(x + d, NX)
        xsend[d - 1] = direction(px).astype(BF)
        cp = remote(xsend.at[d - 1], xrecv.at[d - 1], xs.at[d - 1], xr.at[d - 1], dev(x_=px))
        cp.start()
        xsends.append(cp)
    xsum[...] = direction(x)
    for d in xorder:
        remote(xrecv.at[d - 1], xrecv.at[d - 1], xs.at[d - 1], xr.at[d - 1], sibling).wait_recv()
    total = xsum[...]
    for d in range(1, NX):
        total = total + xrecv[d - 1].astype(F32)
    xsum[...] = total
    ysend[...] = total.astype(BF)

    yorder = [4, 3, 5, 2, 6, 1, 7]
    for d in yorder:
        py = lax.rem(y + d, NY)
        go(remote(ysend.at[rows(py * YR, YR)], yrecv.at[d - 1], ys.at[d - 1], yr.at[d - 1], dev(y_=py)))
    for d in yorder:
        remote(yrecv.at[d - 1], yrecv.at[d - 1], ys.at[d - 1], yr.at[d - 1], sibling).wait_recv()
    total = xsum[rows(y * YR, YR), :]
    for d in range(1, NY):
        total = total + yrecv[d - 1].astype(F32)

    zbuf[zh] = total.astype(BF)
    for d in range(1, NZH):
        go(remote(zbuf.at[zh], zbuf.at[zh], zs.at[d - 1], zr.at[d - 1], dev(zh_=lax.rem(zh + d, NZH))))
    for d in range(1, NZH):
        frm = lax.rem(zh + NZH - d, NZH)
        remote(zbuf.at[frm], zbuf.at[frm], zs.at[d - 1], zr.at[d - 1], sibling).wait_recv()
    total = zbuf[0].astype(F32)
    for i in range(1, NZH):
        total = total + zbuf[i].astype(F32)

    mine = rows(x * XR + y * YR, YR)
    mean[mine, :] = (total * (1.0 / NREP)).astype(BF)
    for d in yorder:
        py = lax.rem(y + d, NY)
        go(remote(mean.at[mine], mean.at[mine], gs.at[d - 1], gr.at[d - 1], dev(y_=py)))
    for d in yorder:
        frm = rows(x * XR + lax.rem(y + NY - d, NY) * YR, YR)
        remote(mean.at[frm], mean.at[frm], gs.at[d - 1], gr.at[d - 1], sibling).wait_recv()
    block = rows(x * XR, XR)
    for d in xorder:
        px = lax.rem(x + d, NX)
        go(remote(mean.at[block], mean.at[block], hs.at[d - 1], hr.at[d - 1], dev(x_=px)))
    for d in xorder:
        frm = rows(lax.rem(x + NX - d, NX) * XR, XR)
        remote(mean.at[frm], mean.at[frm], hs.at[d - 1], hr.at[d - 1], sibling).wait_recv()
    out_ref[...] = mean[...]

    for cp in sends + tsends + xsends:
        cp.wait_send()
    vcopy(f, 6, sibling).wait_send()

    @pl.when(zl < NZL - 1)
    def _():
        vcopy(f, 0, right_f).wait_send()

    @pl.when(zl > 0)
    def _():
        vcopy(f, 3, left_f).wait_send()

    for h in range(1, NZL):
        @pl.when(zl >= h)
        def _():
            slot = f - 2 * h
            if h < NZL - 1:
                @pl.when(zl < NZL - 1)
                def _():
                    vcopy(slot, h, right_f).wait_send()
            vcopy(slot, 6 + h, sibling).wait_send()

        @pl.when(zl + h < NZL)
        def _():
            slot = f + 2 * h
            if h < NZL - 1:
                @pl.when(zl > 0)
                def _():
                    vcopy(slot, 3 + h, left_f).wait_send()
            vcopy(slot, 9 + h, sibling).wait_send()


def step(tokens, queries, keys, targets, weights, m1, m2):
    dma = pltpu.SemaphoreType.DMA
    V = pltpu.VMEM
    return pl.pallas_call(
        kernel,
        out_shape=jax.ShapeDtypeStruct((ROWS, KVW), BF),
        in_specs=[pl.BlockSpec(memory_space=pl.ANY)] * 7,
        out_specs=pl.BlockSpec(memory_space=pltpu.VMEM),
        scratch_shapes=[
            V((SEQ, D), BF), V((SEQ, 2048), BF), V((SEQ, KVW), BF), V((SEQ, 2048), BF),
            V((ROWS, KVW), F32), V((ROWS, KVW), F32), V((ROWS, KVW), F32),
            V((NF, ROWS, KVW), BF), V((NF * SEQ, ROWS), BF), V((NF * SEQ, KVW), BF),
            V((GROUPS, HPG * SEQ, SEQ), BF), V((SEQ, KVW), F32), V((8, 128), F32),
            V((NX - 1, XR, KVW), BF), V((NX - 1, XR, KVW), BF), V((XR, KVW), F32),
            V((XR, KVW), BF), V((NY - 1, YR, KVW), BF), V((NZH, YR, KVW), BF), V((ROWS, KVW), BF),
            dma((7,)), dma((11,)), dma((11,)), dma((7,)), dma((7,)), dma((13,)), dma((13,)),
            dma((3,)), dma((3,)), dma((7,)), dma((7,)), dma((2,)), dma((2,)),
            dma((7,)), dma((7,)), dma((3,)), dma((3,)),
        ],
        compiler_params=pltpu.CompilerParams(
            collective_id=0, has_side_effects=True, vmem_limit_bytes=58 << 20
        ),
    )(tokens, queries, keys, targets, weights, m1, m2)


def per_device(
    tokens, queries, rotated_key_rows, targets, value_weights, momentum, first_moment, second_moment
):
    mean = step(
        tokens, queries, rotated_key_rows, targets, value_weights, first_moment[0], second_moment[0]
    )
    mean_direction = mean.astype(F32) + weight_decay * value_weights
    new_momentum = momentum_keep * momentum + mean_direction
    new_weights = value_weights - outer_rate * inner_rate * (
        mean_direction + momentum_keep * new_momentum
    )
    return (new_weights, new_momentum)


def solution(mesh):
    in_specs = (
        P(("rep", "fsdp"), None),
        P(("rep", "fsdp"), None),
        P(("rep", "fsdp"), None),
        P(("rep", "fsdp"), None),
        P("fsdp", None),
        P("fsdp", None),
        P("rep", "fsdp", None),
        P("rep", "fsdp", None),
    )
    out_specs = (P("fsdp", None), P("fsdp", None))
    return jax.shard_map(
        per_device, mesh=mesh, in_specs=in_specs, out_specs=out_specs, check_vma=False
    )
```

time: 1370 us -> 106 us (0.08)
  the two profiles are of different devices: /device:TPU:62 before, /device:TPU:1 now
where the time goes in v1:
time: 106 us
  Pallas kernels  103 us (97%)
  other arithmetic  2.68 us (3%)
    pallas_call x1, Pallas kernels, step(): pl.pallas_call(kernel, out_shape=jax.ShapeDtypeStruct((ROWS, KVW), BF), i...  103 us
    sub x1, other arithmetic, per_device(): value_weights - outer_rate * inner_rate * (mean_direction + momentum_keep...  2.68 us

profile of v1, /device:TPU:1, one launch (start us, length us, event | category | flops | bytes accessed | tf_op | source)
XLA Modules:
  0.0 106.2 jit_solution(4680854592280061179)
XLA Ops:
  0.6 0.0 copy-start
  0.6 0.0 copy-start.1
  0.7 102.8 %shard_map.95 = bf16[512,512]{1,0:T(8,128)(2,1)} custom-call(bf16[128,4096]{1,0:T(8,128)(2,1)} %tok_h.1, bf16[128,2048]{1,0:T(8,128)(2,1)} %q_h.1, bf16[128,512]{1,0:T(8,128)(2,1)} %k_h.1, bf16[128,2048]{1,0:T(8,128)(2,1)} %t_h.1, f32[512,512]{1,0:T(8,128)} %w_h.1, f32[512,512]{1,0:T(8,128)} %bitcast.2, f32[512,512]{1,0:T(8,128)} %bitcast.3), custom_call_target="tpu_custom_call" | custom-call | tf_op jit(solution)/shard_map/pallas_call | solution.py:371
  103.5 0.0 copy-done
  103.5 0.0 copy-done.1
  103.5 2.7 %multiply_subtract_fusion = (f32[512,512]{1,0:T(8,128)}, f32[512,512]{1,0:T(8,128)}) fusion(f32[512,512]{1,0:T(8,128)S(1)} %copy-done, bf16[512,512]{1,0:T(8,128)(2,1)} %shard_map.95, f32[512,512]{1,0:T(8,128)S(1)} %copy-done.1), kind=kLoop, calls=%fused_computation | loop fusion | flops 2359296 | bytes 4718592 | tf_op jit(solution)/shard_map/sub | solution.py:401
Async XLA Ops:
  0.6 102.9 %copy-start = (f32[512,512]{1,0:T(8,128)S(1)}, f32[512,512]{1,0:T(8,128)}, u32[]{:S(2)}) copy-start(f32[512,512]{1,0:T(8,128)} %w_h.1) | copy-start | bytes 3145732
  0.6 102.9 %copy-start.1 = (f32[512,512]{1,0:T(8,128)S(1)}, f32[512,512]{1,0:T(8,128)}, u32[]{:S(2)}) copy-start(f32[512,512]{1,0:T(8,128)} %param.13) | copy-start | bytes 3145732

commit v2 on v0

v2 whole, which is shorter than its diff:
```python
import math

import jax
import jax.numpy as jnp
from jax import lax
from jax.experimental import pallas as pl
from jax.experimental.pallas import tpu as pltpu
from jax.sharding import PartitionSpec as P

D = 4096
HEAD = 128
NX, NY, NZH, NZL = 4, 8, 3, 4
NREP = NX * NY * NZH
NF = 8
SEQ = 128
KVW = 512
ROWS = 512
GROUPS = 4
HPG = 4
XR = ROWS // NX
YR = XR // NY
MESH = pl.DeviceIdType.MESH
BF = jnp.bfloat16
F32 = jnp.float32

first_decay = 0.9
second_decay = 0.95
weight_decay = 0.1
inner_rate = 0.05
outer_rate = 0.7
momentum_keep = 0.9
epsilon = 1e-08


def rows(start, size):
    return pl.ds(pl.multiple_of(start, size), size)


HALF = ROWS // 2
RA = ROWS * 3 // 4
XS = RA // NX
YS = (ROWS - RA) // NY
CH = KVW // 2
CA = KVW * 3 // 4
CB = KVW - CA
BR = ROWS // NY
PW = ROWS // 2


def kernel(
    tok_h, q_h, k_h, t_h, w_h, m1_h, m2_h, out_ref,
    tok, q, k, t, w, m1, m2,
    wall, tokc, vgall, probs, acc, dirs, dsend_a, dsend_b,
    recv1a, recv1b, sum_a, sum_b, send_a, send_b, recv2a, recv2b, zbuf, mean_a, mean_b,
    loc, lt, wz, wx, wy, wd, ts, vs, r1a, r1b, r2a, r2b, rz, g1a, g1b, g2a, g2b,
):
    r = lax.axis_index("rep")
    f = lax.axis_index("fsdp")
    zh = lax.div(r, NX * NY)
    x = lax.rem(lax.div(r, NY), NX)
    y = lax.rem(r, NY)
    zl = lax.div(f, 2)
    c = lax.rem(f, 2)

    def dev(zh_=zh, x_=x, y_=y, f_=f):
        return {"rep": zh_ * (NX * NY) + x_ * NY + y_, "fsdp": f_}

    def along(d):
        zp = lax.rem(zh * NZL + zl + d + NZH * NZL, NZH * NZL)
        return dev(zh_=lax.div(zp, NZL), f_=lax.rem(zp, NZL) * 2 + c)

    sib = f + 1 - 2 * c
    sibling = dev(f_=sib)
    right, left, right2, left2 = along(1), along(-1), along(2), along(-2)
    x_r, x_l = dev(x_=lax.rem(x + 1, NX)), dev(x_=lax.rem(x + NX - 1, NX))
    y_r, y_l = dev(y_=lax.rem(y + 1, NY)), dev(y_=lax.rem(y + NY - 1, NY))

    loads = [pltpu.make_async_copy(w_h, w, loc.at[0])]
    loads[0].start()

    barrier = pltpu.get_barrier_semaphore()
    peers = [right, left, right2, left2]
    peers += [dev(f_=lax.rem(f + d, NF)) for d in range(1, NF)]
    peers += [dev(x_=lax.rem(x + d, NX)) for d in range(1, NX)]
    peers += [dev(y_=lax.rem(y + d, NY)) for d in range(1, NY)]
    peers += [dev(zh_=lax.rem(zh + d, NZH)) for d in range(1, NZH)]
    for p in peers:
        pl.semaphore_signal(barrier, inc=1, device_id=p, device_id_type=MESH)

    tloads = []
    for j in range(D // PW):
        ct = pltpu.make_async_copy(tok_h.at[:, pl.ds(j * PW, PW)], tok.at[j], lt.at[j])
        ct.start()
        tloads.append(ct)
    for i, (src, dst) in enumerate([(q_h, q), (k_h, k), (t_h, t), (m1_h, m1), (m2_h, m2)]):
        cp = pltpu.make_async_copy(src, dst, loc.at[i + 1])
        cp.start()
        loads.append(cp)

    loads[0].wait()
    wall[f] = w[...].astype(BF)
    pl.semaphore_wait(barrier, len(peers))

    def remote(src, dst, sem, i, to):
        return pltpu.make_async_remote_copy(
            src_ref=src, dst_ref=dst, send_sem=sem.at[0, i], recv_sem=sem.at[1, i],
            device_id=to, device_id_type=MESH,
        )

    sends = []

    def go(ref, sem, i, to, dst=None):
        cp = remote(ref, ref if dst is None else dst, sem, i, to)
        cp.start()
        sends.append(cp)

    def got(ref, sem, i):
        remote(ref, ref, sem, i, sibling).wait_recv()

    f_l = lax.rem(zl + NZL - 1, NZL) * 2 + c
    f_r = lax.rem(zl + 1, NZL) * 2 + c
    f_o = lax.rem(zl + 2, NZL) * 2 + c
    slots = [f_l, f_r, f_o]

    def wa(s, p, h=None):
        if h is None:
            return wall.at[s, rows(p * XS, XS)]
        return wall.at[s, rows(p * XS + h * (XS // 2), XS // 2)]

    def wb(s, p):
        return wall.at[s, rows(RA + p * YS, YS)]

    def at_x(d):
        return lax.rem(x + d + NX, NX)

    def at_y(d):
        return lax.rem(y + d + NY, NY)

    far_y = [4, 3, 5, 2, 6, 1, 7]
    far_x = [2, 1, 3]

    go(wa(f, x), wz, 0, right)
    go(wb(f, y), wz, 1, right)
    go(wa(f, x), wz, 2, left)
    go(wb(f, y), wz, 3, left)
    go(wa(f, x), wz, 4, right2)
    go(wb(f, y), wz, 5, left2)
    go(wall.at[f], wd, 0, sibling)

    px = lax.div(x, 2)
    pairs = [1 - px, px]
    TH = SEQ // 2

    def tparts(n):
        to = lax.rem(f + n, NF)
        frm = lax.rem(f + NF - n, NF)
        whole = (tok.at[2 * to + pairs[0]], tokc.at[pairs[0], rows(f * SEQ, SEQ)],
                 tokc.at[pairs[0], rows(frm * SEQ, SEQ)])
        halves = [
            (tok.at[2 * to + pairs[1], pl.ds(h * TH, TH)],
             tokc.at[pairs[1], rows(f * SEQ + h * TH, TH)],
             tokc.at[pairs[1], rows(frm * SEQ + h * TH, TH)])
            for h in range(2)
        ]
        return [whole] + halves

    def tsend(part):
        for n in range(1, NF):
            src, dst, _ = tparts(n)[part]
            go(src, ts, part * 7 + n - 1, dev(f_=lax.rem(f + n, NF)), dst=dst)

    def tgot(part):
        for n in range(1, NF):
            got(tparts(n)[part][2], ts, part * 7 + n - 1)

    for ct in tloads:
        ct.wait()
    tsend(0)
    tsend(1)
    for m in range(2):
        tokc[m, rows(f * SEQ, SEQ), :] = tok[2 * f + m]

    loads[1].wait()
    loads[2].wait()
    causal = lax.broadcasted_iota(jnp.int32, (SEQ, SEQ), 0) >= lax.broadcasted_iota(
        jnp.int32, (SEQ, SEQ), 1
    )
    score_scale = 1.0 / math.sqrt(HEAD)

    def scores_of(g):
        kg = k[:, g * HEAD : (g + 1) * HEAD]
        for j in range(HPG):
            h = g * HPG + j
            s = lax.dot_general(
                q[:, h * HEAD : (h + 1) * HEAD], kg, (((1,), (1,)), ((), ())),
                preferred_element_type=F32,
            )
            s = jnp.where(causal, s * score_scale, -jnp.inf)
            e = jnp.exp(s - jnp.max(s, axis=-1, keepdims=True))
            p = e / jnp.sum(e, axis=-1, keepdims=True)
            probs[g, j * SEQ : (j + 1) * SEQ, :] = p.astype(BF)

    for g in range(2):
        scores_of(g)

    for n, s in enumerate(slots):
        got(wa(s, x), wz, 2 * n)
        go(wa(s, x), wx, n, x_r)
        go(wa(s, x), wx, 3 + n, x_l)
        got(wb(s, y), wz, 2 * n + 1)
        for d in far_y:
            go(wb(s, y), wy, n * 7 + d - 1, dev(y_=at_y(d)))

    def term(slot, h):
        return jnp.dot(
            tok[2 * slot + h], wall[slot, h * HALF : (h + 1) * HALF, :],
            preferred_element_type=F32,
        )

    acc[...] = term(f, 0) + term(f, 1)
    scores_of(2)
    for n, s in enumerate(slots):
        got(wa(s, at_x(-1)), wx, n)
        go(wa(s, at_x(-1), 0), wx, 6 + n, x_r)
        got(wa(s, at_x(1)), wx, 3 + n)
        go(wa(s, at_x(1), 1), wx, 9 + n, x_l)
    scores_of(3)
    got(wall.at[sib], wd, 0)
    acc[...] += term(sib, 0) + term(sib, 1)

    def part(s, h):
        return wall.at[s, pl.ds(0, RA)] if h == 0 else wall.at[s, pl.ds(RA, ROWS - RA)]

    for n, s in enumerate(slots):
        for d in far_y:
            got(wb(s, at_y(-d)), wy, n * 7 + d - 1)
        go(part(s, 1), wd, 4 + n, sibling)
    for n, s in enumerate(slots):
        got(wa(s, at_x(2), 0), wx, 6 + n)
        got(wa(s, at_x(2), 1), wx, 9 + n)
        go(part(s, 0), wd, 1 + n, sibling)
        acc[...] += term(s, 0) + term(s, 1)
    for n, s in enumerate(slots):
        o = s + 1 - 2 * c
        got(part(o, 1), wd, 4 + n)
        got(part(o, 0), wd, 1 + n)
        acc[...] += term(o, 0) + term(o, 1)

    inv_root = 1.0 / math.sqrt(D)
    cot_scale = math.sqrt(D / (SEQ * NF))
    loads[3].wait()

    def value_grad_of(g):
        cols = slice(g * HEAD, (g + 1) * HEAD)
        v = (acc[:, cols] * inv_root).astype(BF)
        o = jnp.dot(probs[g], v, preferred_element_type=F32)
        tg = jnp.concatenate(
            [t[:, (g * HPG + j) * HEAD : (g * HPG + j + 1) * HEAD] for j in range(HPG)], axis=0
        )
        res = ((o - tg.astype(F32)) * cot_scale).astype(BF)
        vg = lax.dot_general(probs[g], res, (((0,), (0,)), ((), ())), preferred_element_type=F32)
        vgall[g // 2, rows(f * SEQ, SEQ), (g % 2) * HEAD : (g % 2 + 1) * HEAD] = vg.astype(BF)

    def vcopy(slot, i, ch, to):
        ref = vgall.at[ch, rows(slot * SEQ, SEQ)]
        return remote(ref, ref, vs, ch * 13 + i, to)

    right_f = dev(f_=jnp.minimum(f + 2, NF - 2 + c))
    left_f = dev(f_=jnp.maximum(f - 2, c))

    def own_copies(ch, act):
        act(vcopy(f, 6, ch, sibling))

        @pl.when(zl < NZL - 1)
        def _():
            act(vcopy(f, 0, ch, right_f))

        @pl.when(zl > 0)
        def _():
            act(vcopy(f, 3, ch, left_f))

    def relay(h, ch, act, wait):
        @pl.when(zl >= h)
        def _():
            slot = f - 2 * h
            if wait:
                vcopy(slot, h - 1, ch, sibling).wait_recv()
            if h < NZL - 1:
                @pl.when(zl < NZL - 1)
                def _():
                    act(vcopy(slot, h, ch, right_f))
            act(vcopy(slot, 6 + h, ch, sibling))

        @pl.when(zl + h < NZL)
        def _():
            slot = f + 2 * h
            if wait:
                vcopy(slot, 3 + h - 1, ch, sibling).wait_recv()
            if h < NZL - 1:
                @pl.when(zl > 0)
                def _():
                    act(vcopy(slot, 3 + h, ch, left_f))
            act(vcopy(slot, 9 + h, ch, sibling))

    def start(cp):
        cp.start()

    def sent(cp):
        cp.wait_send()

    for ch in range(2):
        value_grad_of(2 * ch)
        value_grad_of(2 * ch + 1)
        own_copies(ch, start)
    for h in range(1, NZL):
        for ch in range(2):
            relay(h, ch, start, True)
    tsend(2)

    def sibling_got(ch):
        vcopy(sib, 6, ch, sibling).wait_recv()
        for h in range(1, NZL):
            @pl.when(zl >= h)
            def _():
                vcopy(sib - 2 * h, 6 + h, ch, sibling).wait_recv()

            @pl.when(zl + h < NZL)
            def _():
                vcopy(sib + 2 * h, 9 + h, ch, sibling).wait_recv()

    for ch in range(2):
        sibling_got(ch)
    loads[4].wait()
    loads[5].wait()

    A, B = slice(0, CA), slice(CA, KVW)

    def direction(m, e):
        n = 2 * m + e
        at = rows(n * XR, XR)
        for ch in range(2):
            cols = slice(ch * CH, (ch + 1) * CH)
            grad = lax.dot_general(
                tokc[m, :, rows(e * XR, XR)], vgall[ch], (((0,), (0,)), ((), ())),
                preferred_element_type=F32,
            ) * inv_root
            fn = first_decay * m1[at, cols] + (1.0 - first_decay) * grad
            sn = second_decay * m2[at, cols] + (1.0 - second_decay) * grad * grad
            dirs[at, cols] = fn / (jnp.sqrt(sn) + epsilon)
        d = dirs[at, :]
        dsend_a[at, :] = d[:, A].astype(BF)
        dsend_b[at, :] = d[:, B].astype(BF)
        return n

    b = lax.rem(x, 2)
    ysends = []
    for i, (m, e) in enumerate([(1 - px, b), (1 - px, 1 - b), (px, 1 - b), (px, b)]):
        if i == 0:
            tgot(0)
        if i == 2:
            tgot(1)
            tgot(2)
        n = direction(m, e)
        if i < 3:
            go(dsend_a.at[rows(n * XR, XR)], r1a, i, dev(x_=n), dst=recv1a.at[i])
        for u in range(2):
            to = 2 * n + u
            j = lax.rem(to - y + NY, NY)
            cp = remote(dsend_b.at[rows(to * BR, BR)], recv1b.at[j], r1b, j, dev(y_=to))
            ysends.append((to, cp))

            @pl.when(to != y)
            def _():
                cp.start()

    for i in range(3):
        got(recv1a.at[i], r1a, i)
    total = dirs[rows(x * XR, XR), A]
    for i in range(3):
        total = total + recv1a[i].astype(F32)
    sum_a[...] = total
    send_a[...] = total.astype(BF)
    for d in far_y:
        go(send_a.at[rows(at_y(d) * YR, YR)], r2a, d - 1, dev(y_=at_y(d)), dst=recv2a.at[d - 1])
    for d in range(1, NY):
        got(recv1b.at[d], r1b, d)
    total = dirs[rows(y * BR, BR), B]
    for d in range(1, NY):
        total = total + recv1b[d].astype(F32)
    sum_b[...] = total
    send_b[...] = total.astype(BF)
    for d in far_x:
        go(send_b.at[rows(at_x(d) * YR, YR)], r2b, d - 1, dev(x_=at_x(d)), dst=recv2b.at[d - 1])
    for d in range(1, NY):
        got(recv2a.at[d - 1], r2a, d - 1)
    total = sum_a[rows(y * YR, YR), :]
    for d in range(1, NY):
        total = total + recv2a[d - 1].astype(F32)
    zbuf[zh, :, A] = total.astype(BF)
    for d in range(1, NX):
        got(recv2b.at[d - 1], r2b, d - 1)
    total = sum_b[rows(x * YR, YR), :]
    for d in range(1, NX):
        total = total + recv2b[d - 1].astype(F32)
    zbuf[zh, :, B] = total.astype(BF)

    for d in range(1, NZH):
        go(zbuf.at[zh], rz, d - 1, dev(zh_=lax.rem(zh + d, NZH)))
    for d in range(1, NZH):
        got(zbuf.at[lax.rem(zh + NZH - d, NZH)], rz, d - 1)

    def spot_a(x_, y_):
        return mean_a.at[rows(x_ * XR + y_ * YR, YR)]

    def spot_b(x_, y_):
        return mean_b.at[rows(y_ * BR + x_ * YR, YR)]

    total = zbuf[0].astype(F32)
    for z in range(1, NZH):
        total = total + zbuf[z].astype(F32)
    piece = (total * (1.0 / NREP)).astype(BF)
    mean_a[rows(x * XR + y * YR, YR), :] = piece[:, A]
    for d in far_y:
        go(spot_a(x, y), g1a, d - 1, dev(y_=at_y(d)))
    mean_b[rows(y * BR + x * YR, YR), :] = piece[:, B]
    for d in far_x:
        go(spot_b(x, y), g1b, d - 1, dev(x_=at_x(d)))
    for d in far_x:
        got(spot_b(at_x(-d), y), g1b, d - 1)
    for d in far_y:
        go(mean_b.at[rows(y * BR, BR)], g2b, d - 1, dev(y_=at_y(d)))
    for d in far_y:
        got(spot_a(x, at_y(-d)), g1a, d - 1)
    for d in far_x:
        go(mean_a.at[rows(x * XR, XR)], g2a, d - 1, dev(x_=at_x(d)))
    for d in far_y:
        got(mean_b.at[rows(at_y(-d) * BR, BR)], g2b, d - 1)
    out_ref[:, B] = mean_b[...]
    for d in far_x:
        got(mean_a.at[rows(at_x(-d) * XR, XR)], g2a, d - 1)
    out_ref[:, A] = mean_a[...]

    for cp in sends:
        cp.wait_send()
    for to, cp in ysends:
        @pl.when(to != y)
        def _():
            cp.wait_send()
    for ch in range(2):
        own_copies(ch, sent)
        for h in range(1, NZL):
            relay(h, ch, sent, False)


def step(tokens, queries, keys, targets, weights, m1, m2):
    def dma(n):
        return pltpu.SemaphoreType.DMA((2, n))

    V = pltpu.VMEM
    return pl.pallas_call(
        kernel,
        out_shape=jax.ShapeDtypeStruct((ROWS, KVW), BF),
        in_specs=[pl.BlockSpec(memory_space=pl.ANY)] * 7,
        out_specs=pl.BlockSpec(memory_space=pltpu.VMEM),
        scratch_shapes=[
            V((D // PW, SEQ, PW), BF), V((SEQ, 2048), BF), V((SEQ, KVW), BF), V((SEQ, 2048), BF),
            V((ROWS, KVW), F32), V((ROWS, KVW), F32), V((ROWS, KVW), F32),
            V((NF, ROWS, KVW), BF), V((2, NF * SEQ, PW), BF), V((2, NF * SEQ, CH), BF),
            V((GROUPS, HPG * SEQ, SEQ), BF), V((SEQ, KVW), F32),
            V((ROWS, KVW), F32), V((ROWS, CA), BF), V((ROWS, CB), BF),
            V((NX - 1, XR, CA), BF), V((NY, BR, CB), BF),
            V((XR, CA), F32), V((BR, CB), F32), V((XR, CA), BF), V((BR, CB), BF),
            V((NY - 1, YR, CA), BF), V((NX - 1, YR, CB), BF),
            V((NZH, YR, KVW), BF), V((ROWS, CA), BF), V((ROWS, CB), BF),
            pltpu.SemaphoreType.DMA((6,)), pltpu.SemaphoreType.DMA((D // PW,)),
            dma(6), dma(12), dma(21), dma(7), dma(21), dma(26),
            dma(3), dma(8), dma(7), dma(3), dma(2), dma(7), dma(3), dma(3), dma(7),
        ],
        compiler_params=pltpu.CompilerParams(
            collective_id=0, has_side_effects=True, vmem_limit_bytes=58 << 20
        ),
    )(tokens, queries, keys, targets, weights, m1, m2)


def per_device(
    tokens, queries, rotated_key_rows, targets, value_weights, momentum, first_moment, second_moment
):
    mean = step(
        tokens, queries, rotated_key_rows, targets, value_weights, first_moment[0], second_moment[0]
    )
    mean_direction = mean.astype(F32) + weight_decay * value_weights
    new_momentum = momentum_keep * momentum + mean_direction
    new_weights = value_weights - outer_rate * inner_rate * (
        mean_direction + momentum_keep * new_momentum
    )
    return (new_weights, new_momentum)


def solution(mesh):
    in_specs = (
        P(("rep", "fsdp"), None),
        P(("rep", "fsdp"), None),
        P(("rep", "fsdp"), None),
        P(("rep", "fsdp"), None),
        P("fsdp", None),
        P("fsdp", None),
        P("rep", "fsdp", None),
        P("rep", "fsdp", None),
    )
    out_specs = (P("fsdp", None), P("fsdp", None))
    return jax.shard_map(
        per_device, mesh=mesh, in_specs=in_specs, out_specs=out_specs, check_vma=False
    )
```

time: 1370 us -> 89.1 us (0.07)
  the two profiles are of different devices: /device:TPU:62 before, /device:TPU:2 now
where the time goes in v2:
time: 89.1 us; the launch traced here: 89 us
  Pallas kernels  85.6 us (96%)
  other arithmetic  2.68 us (3%)
    pallas_call x1, Pallas kernels, step(): pl.pallas_call(kernel, out_shape=jax.ShapeDtypeStruct((ROWS, KVW), BF), i...  85.6 us
    sub x1, other arithmetic, per_device(): value_weights - outer_rate * inner_rate * (mean_direction + momentum_keep...  2.68 us

profile of v2, /device:TPU:2, one launch (start us, length us, event | category | flops | bytes accessed | tf_op | source)
XLA Modules:
  0.0 89.0 jit_solution(12352697795202892180)
XLA Ops:
  0.6 0.0 copy-start
  0.6 0.0 copy-start.1
  0.7 85.6 %shard_map.95 = bf16[512,512]{1,0:T(8,128)(2,1)} custom-call(bf16[128,4096]{1,0:T(8,128)(2,1)} %tok_h.1, bf16[128,2048]{1,0:T(8,128)(2,1)} %q_h.1, bf16[128,512]{1,0:T(8,128)(2,1)} %k_h.1, bf16[128,2048]{1,0:T(8,128)(2,1)} %t_h.1, f32[512,512]{1,0:T(8,128)} %w_h.1, f32[512,512]{1,0:T(8,128)} %bitcast.2, f32[512,512]{1,0:T(8,128)} %bitcast.3), custom_call_target="tpu_custom_call" | custom-call | tf_op jit(solution)/shard_map/pallas_call | solution.py:460
  86.3 0.0 copy-done
  86.3 0.0 copy-done.1
  86.3 2.7 %multiply_subtract_fusion = (f32[512,512]{1,0:T(8,128)}, f32[512,512]{1,0:T(8,128)}) fusion(f32[512,512]{1,0:T(8,128)S(1)} %copy-done, bf16[512,512]{1,0:T(8,128)(2,1)} %shard_map.95, f32[512,512]{1,0:T(8,128)S(1)} %copy-done.1), kind=kLoop, calls=%fused_computation | loop fusion | flops 2359296 | bytes 4718592 | tf_op jit(solution)/shard_map/sub | solution.py:493
Async XLA Ops:
  0.6 85.6 %copy-start = (f32[512,512]{1,0:T(8,128)S(1)}, f32[512,512]{1,0:T(8,128)}, u32[]{:S(2)}) copy-start(f32[512,512]{1,0:T(8,128)} %w_h.1) | copy-start | bytes 3145732
  0.6 85.6 %copy-start.1 = (f32[512,512]{1,0:T(8,128)S(1)}, f32[512,512]{1,0:T(8,128)}, u32[]{:S(2)}) copy-start(f32[512,512]{1,0:T(8,128)} %param.13) | copy-start | bytes 3145732

commit v3 on v2

--- a/solution.py
+++ b/solution.py
@@ -51,8 +51,8 @@
     tok_h, q_h, k_h, t_h, w_h, m1_h, m2_h, out_ref,
     tok, q, k, t, w, m1, m2,
     wall, tokc, vgall, probs, acc, dirs, dsend_a, dsend_b,
-    recv1a, recv1b, sum_a, sum_b, send_a, send_b, recv2a, recv2b, zbuf, mean_a, mean_b,
-    loc, lt, wz, wx, wy, wd, ts, vs, r1a, r1b, r2a, r2b, rz, g1a, g1b, g2a, g2b,
+    recv1a, recv1b, sum_a, sum_b, send_a, send_b, recv2a, recv2b, zbuf, mean_a, mean_b, w_a, w_b, wz_a, wz_b,
+    loc, lw, lt, wz, wx, wy, wd, ts, vs, r1a, r1b, r2a, r2b, rz, g1a, g1b, g2a, g2b,
 ):
     r = lax.axis_index("rep")
     f = lax.axis_index("fsdp")
@@ -76,6 +76,13 @@
     y_r, y_l = dev(y_=lax.rem(y + 1, NY)), dev(y_=lax.rem(y + NY - 1, NY))
 
     loads = [pltpu.make_async_copy(w_h, w, loc.at[0])]
+    at_a, at_b = rows(x * XS, XS), rows(RA + y * YS, YS)
+    first = [
+        pltpu.make_async_copy(w_h.at[at_a], w_a, lw.at[0]),
+        pltpu.make_async_copy(w_h.at[at_b], w_b, lw.at[1]),
+    ]
+    for cp in first:
+        cp.start()
     loads[0].start()
 
     barrier = pltpu.get_barrier_semaphore()
@@ -87,6 +94,66 @@
     for p in peers:
         pl.semaphore_signal(barrier, inc=1, device_id=p, device_id_type=MESH)
 
+    for cp in first:
+        cp.wait()
+    wz_a[...] = w_a[...].astype(BF)
+    wz_b[...] = w_b[...].astype(BF)
+    pl.semaphore_wait(barrier, len(peers))
+
+    def remote(src, dst, sem, i, to):
+        return pltpu.make_async_remote_copy(
+            src_ref=src, dst_ref=dst, send_sem=sem.at[0, i], recv_sem=sem.at[1, i],
+            device_id=to, device_id_type=MESH,
+        )
+
+    sends = []
+
+    def go(ref, sem, i, to, dst=None):
+        cp = remote(ref, ref if dst is None else dst, sem, i, to)
+        cp.start()
+        sends.append(cp)
+
+    def got(ref, sem, i):
+        remote(ref, ref, sem, i, sibling).wait_recv()
+
+    def many(copies, whole, sem, i):
+        for src, dst, to in copies:
+            remote(src, dst, sem, i, to).start()
+        sends.append(remote(whole, whole, sem, i, sibling))
+
+    def flush():
+        for cp in sends:
+            cp.wait_send()
+        sends.clear()
+
+    f_l = lax.rem(zl + NZL - 1, NZL) * 2 + c
+    f_r = lax.rem(zl + 1, NZL) * 2 + c
+    f_o = lax.rem(zl + 2, NZL) * 2 + c
+    slots = [f_l, f_r, f_o]
+
+    def wa(s, p, h=None):
+        if h is None:
+            return wall.at[s, rows(p * XS, XS)]
+        return wall.at[s, rows(p * XS + h * (XS // 2), XS // 2)]
+
+    def wb(s, p):
+        return wall.at[s, rows(RA + p * YS, YS)]
+
+    def at_x(d):
+        return lax.rem(x + d + NX, NX)
+
+    def at_y(d):
+        return lax.rem(y + d + NY, NY)
+
+    far_y = [4, 3, 5, 2, 6, 1, 7]
+    far_x = [2, 1, 3]
+
+    go(wz_a, wz, 0, right, dst=wa(f, x))
+    go(wz_a, wz, 2, left, dst=wa(f, x))
+    go(wz_a, wz, 4, right2, dst=wa(f, x))
+    go(wz_b, wz, 5, left2, dst=wb(f, y))
+    go(wz_b, wz, 1, right, dst=wb(f, y))
+    go(wz_b, wz, 3, left, dst=wb(f, y))
     tloads = []
     for j in range(D // PW):
         ct = pltpu.make_async_copy(tok_h.at[:, pl.ds(j * PW, PW)], tok.at[j], lt.at[j])
@@ -99,79 +166,37 @@
 
     loads[0].wait()
     wall[f] = w[...].astype(BF)
-    pl.semaphore_wait(barrier, len(peers))
-
-    def remote(src, dst, sem, i, to):
-        return pltpu.make_async_remote_copy(
-            src_ref=src, dst_ref=dst, send_sem=sem.at[0, i], recv_sem=sem.at[1, i],
-            device_id=to, device_id_type=MESH,
-        )
-
-    sends = []
-
-    def go(ref, sem, i, to, dst=None):
-        cp = remote(ref, ref if dst is None else dst, sem, i, to)
-        cp.start()
-        sends.append(cp)
-
-    def got(ref, sem, i):
-        remote(ref, ref, sem, i, sibling).wait_recv()
-
-    f_l = lax.rem(zl + NZL - 1, NZL) * 2 + c
-    f_r = lax.rem(zl + 1, NZL) * 2 + c
-    f_o = lax.rem(zl + 2, NZL) * 2 + c
-    slots = [f_l, f_r, f_o]
-
-    def wa(s, p, h=None):
-        if h is None:
-            return wall.at[s, rows(p * XS, XS)]
-        return wall.at[s, rows(p * XS + h * (XS // 2), XS // 2)]
-
-    def wb(s, p):
-        return wall.at[s, rows(RA + p * YS, YS)]
-
-    def at_x(d):
-        return lax.rem(x + d + NX, NX)
-
-    def at_y(d):
-        return lax.rem(y + d + NY, NY)
-
-    far_y = [4, 3, 5, 2, 6, 1, 7]
-    far_x = [2, 1, 3]
-
-    go(wa(f, x), wz, 0, right)
-    go(wb(f, y), wz, 1, right)
-    go(wa(f, x), wz, 2, left)
-    go(wb(f, y), wz, 3, left)
-    go(wa(f, x), wz, 4, right2)
-    go(wb(f, y), wz, 5, left2)
     go(wall.at[f], wd, 0, sibling)
 
     px = lax.div(x, 2)
     pairs = [1 - px, px]
-    TH = SEQ // 2
+    cuts = [(0, SEQ // 2), (SEQ // 2, SEQ // 2)]
 
     def tparts(n):
         to = lax.rem(f + n, NF)
-        frm = lax.rem(f + NF - n, NF)
-        whole = (tok.at[2 * to + pairs[0]], tokc.at[pairs[0], rows(f * SEQ, SEQ)],
-                 tokc.at[pairs[0], rows(frm * SEQ, SEQ)])
+        whole = (tok.at[2 * to + pairs[0]], tokc.at[pairs[0], rows(f * SEQ, SEQ)])
         halves = [
-            (tok.at[2 * to + pairs[1], pl.ds(h * TH, TH)],
-             tokc.at[pairs[1], rows(f * SEQ + h * TH, TH)],
-             tokc.at[pairs[1], rows(frm * SEQ + h * TH, TH)])
-            for h in range(2)
+            (tok.at[2 * to + pairs[1], pl.ds(at, size)],
+             tokc.at[pairs[1], pl.ds(pl.multiple_of(f * SEQ + at, SEQ // 4), size)])
+            for at, size in cuts
         ]
         return [whole] + halves
 
+    twhole = [
+        tokc.at[0, pl.ds(0, (NF - 1) * SEQ)],
+        tokc.at[0, pl.ds(0, (NF - 1) * cuts[0][1])],
+        tokc.at[0, pl.ds(0, (NF - 1) * cuts[1][1])],
+    ]
+
     def tsend(part):
+        copies = []
         for n in range(1, NF):
-            src, dst, _ = tparts(n)[part]
-            go(src, ts, part * 7 + n - 1, dev(f_=lax.rem(f + n, NF)), dst=dst)
+            src, dst = tparts(n)[part]
+            copies.append((src, dst, dev(f_=lax.rem(f + n, NF))))
+        many(copies, twhole[part], ts, part)
 
     def tgot(part):
-        for n in range(1, NF):
-            got(tparts(n)[part][2], ts, part * 7 + n - 1)
+        got(twhole[part], ts, part)
 
     for ct in tloads:
         ct.wait()
@@ -203,13 +228,15 @@
     for g in range(2):
         scores_of(g)
 
+    rest = wall.at[0, pl.ds(0, (NY - 1) * YS)]
+
     for n, s in enumerate(slots):
         got(wa(s, x), wz, 2 * n)
         go(wa(s, x), wx, n, x_r)
         go(wa(s, x), wx, 3 + n, x_l)
         got(wb(s, y), wz, 2 * n + 1)
-        for d in far_y:
-            go(wb(s, y), wy, n * 7 + d - 1, dev(y_=at_y(d)))
+        piece = wb(s, y)
+        many([(piece, piece, dev(y_=at_y(d))) for d in far_y], rest, wy, n)
 
     def term(slot, h):
         return jnp.dot(
@@ -217,13 +244,13 @@
             preferred_element_type=F32,
         )
 
-    acc[...] = term(f, 0) + term(f, 1)
-    scores_of(2)
     for n, s in enumerate(slots):
         got(wa(s, at_x(-1)), wx, n)
         go(wa(s, at_x(-1), 0), wx, 6 + n, x_r)
         got(wa(s, at_x(1)), wx, 3 + n)
         go(wa(s, at_x(1), 1), wx, 9 + n, x_l)
+    acc[...] = term(f, 0) + term(f, 1)
+    scores_of(2)
     scores_of(3)
     got(wall.at[sib], wd, 0)
     acc[...] += term(sib, 0) + term(sib, 1)
@@ -232,8 +259,7 @@
         return wall.at[s, pl.ds(0, RA)] if h == 0 else wall.at[s, pl.ds(RA, ROWS - RA)]
 
     for n, s in enumerate(slots):
-        for d in far_y:
-            got(wb(s, at_y(-d)), wy, n * 7 + d - 1)
+        got(rest, wy, n)
         go(part(s, 1), wd, 4 + n, sibling)
     for n, s in enumerate(slots):
         got(wa(s, at_x(2), 0), wx, 6 + n)
@@ -312,10 +338,12 @@
         value_grad_of(2 * ch)
         value_grad_of(2 * ch + 1)
         own_copies(ch, start)
+    flush()
     for h in range(1, NZL):
         for ch in range(2):
             relay(h, ch, start, True)
-    tsend(2)
+        if h == NZL - 2:
+            tsend(2)
 
     def sibling_got(ch):
         vcopy(sib, 6, ch, sibling).wait_recv()
@@ -353,7 +381,6 @@
         return n
 
     b = lax.rem(x, 2)
-    ysends = []
     for i, (m, e) in enumerate([(1 - px, b), (1 - px, 1 - b), (px, 1 - b), (px, b)]):
         if i == 0:
             tgot(0)
@@ -366,13 +393,18 @@
         for u in range(2):
             to = 2 * n + u
             j = lax.rem(to - y + NY, NY)
-            cp = remote(dsend_b.at[rows(to * BR, BR)], recv1b.at[j], r1b, j, dev(y_=to))
-            ysends.append((to, cp))
+            cp = remote(dsend_b.at[rows(to * BR, BR)], recv1b.at[j], r1b, 0, dev(y_=to))
 
             @pl.when(to != y)
             def _():
                 cp.start()
 
+    b_whole = recv1b.at[pl.ds(0, NY - 1)]
+    sends.append(remote(b_whole, b_whole, r1b, 0, sibling))
+    for ch in range(2):
+        own_copies(ch, sent)
+        for h in range(1, NZL):
+            relay(h, ch, sent, False)
     for i in range(3):
         got(recv1a.at[i], r1a, i)
     total = dirs[rows(x * XR, XR), A]
@@ -380,32 +412,41 @@
         total = total + recv1a[i].astype(F32)
     sum_a[...] = total
     send_a[...] = total.astype(BF)
-    for d in far_y:
-        go(send_a.at[rows(at_y(d) * YR, YR)], r2a, d - 1, dev(y_=at_y(d)), dst=recv2a.at[d - 1])
-    for d in range(1, NY):
-        got(recv1b.at[d], r1b, d)
+    many(
+        [(send_a.at[rows(at_y(d) * YR, YR)], recv2a.at[d - 1], dev(y_=at_y(d))) for d in far_y],
+        recv2a, r2a, 0,
+    )
+    got(b_whole, r1b, 0)
     total = dirs[rows(y * BR, BR), B]
     for d in range(1, NY):
         total = total + recv1b[d].astype(F32)
     sum_b[...] = total
     send_b[...] = total.astype(BF)
-    for d in far_x:
-        go(send_b.at[rows(at_x(d) * YR, YR)], r2b, d - 1, dev(x_=at_x(d)), dst=recv2b.at[d - 1])
-    for d in range(1, NY):
-        got(recv2a.at[d - 1], r2a, d - 1)
+    late = list(sends)
+    sends.clear()
+    many(
+        [(send_b.at[rows(at_x(d) * YR, YR)], recv2b.at[d - 1], dev(x_=at_x(d))) for d in far_x],
+        recv2b, r2b, 0,
+    )
+    for cp in late:
+        cp.wait_send()
+    got(recv2a, r2a, 0)
     total = sum_a[rows(y * YR, YR), :]
     for d in range(1, NY):
         total = total + recv2a[d - 1].astype(F32)
     zbuf[zh, :, A] = total.astype(BF)
-    for d in range(1, NX):
-        got(recv2b.at[d - 1], r2b, d - 1)
+    got(recv2b, r2b, 0)
     total = sum_b[rows(x * YR, YR), :]
     for d in range(1, NX):
         total = total + recv2b[d - 1].astype(F32)
     zbuf[zh, :, B] = total.astype(BF)
 
+    late = list(sends)
+    sends.clear()
     for d in range(1, NZH):
         go(zbuf.at[zh], rz, d - 1, dev(zh_=lax.rem(zh + d, NZH)))
+    for cp in late:
+        cp.wait_send()
     for d in range(1, NZH):
         got(zbuf.at[lax.rem(zh + NZH - d, NZH)], rz, d - 1)
 
@@ -420,36 +461,24 @@
         total = total + zbuf[z].astype(F32)
     piece = (total * (1.0 / NREP)).astype(BF)
     mean_a[rows(x * XR + y * YR, YR), :] = piece[:, A]
-    for d in far_y:
-        go(spot_a(x, y), g1a, d - 1, dev(y_=at_y(d)))
+    a7, a3 = mean_a.at[pl.ds(0, (NY - 1) * YR)], mean_a.at[pl.ds(0, (NX - 1) * XR)]
+    b3, b7 = mean_b.at[pl.ds(0, (NX - 1) * YR)], mean_b.at[pl.ds(0, (NY - 1) * BR)]
+    spot = spot_a(x, y)
+    many([(spot, spot, dev(y_=at_y(d))) for d in far_y], a7, g1a, 0)
     mean_b[rows(y * BR + x * YR, YR), :] = piece[:, B]
-    for d in far_x:
-        go(spot_b(x, y), g1b, d - 1, dev(x_=at_x(d)))
-    for d in far_x:
-        got(spot_b(at_x(-d), y), g1b, d - 1)
-    for d in far_y:
-        go(mean_b.at[rows(y * BR, BR)], g2b, d - 1, dev(y_=at_y(d)))
-    for d in far_y:
-        got(spot_a(x, at_y(-d)), g1a, d - 1)
-    for d in far_x:
-        go(mean_a.at[rows(x * XR, XR)], g2a, d - 1, dev(x_=at_x(d)))
-    for d in far_y:
-        got(mean_b.at[rows(at_y(-d) * BR, BR)], g2b, d - 1)
+    spot = spot_b(x, y)
+    many([(spot, spot, dev(x_=at_x(d))) for d in far_x], b3, g1b, 0)
+    got(b3, g1b, 0)
+    block = mean_b.at[rows(y * BR, BR)]
+    many([(block, block, dev(y_=at_y(d))) for d in far_y], b7, g2b, 0)
+    got(a7, g1a, 0)
+    block = mean_a.at[rows(x * XR, XR)]
+    many([(block, block, dev(x_=at_x(d))) for d in far_x], a3, g2a, 0)
+    flush()
+    got(b7, g2b, 0)
     out_ref[:, B] = mean_b[...]
-    for d in far_x:
-        got(mean_a.at[rows(at_x(-d) * XR, XR)], g2a, d - 1)
+    got(a3, g2a, 0)
     out_ref[:, A] = mean_a[...]
-
-    for cp in sends:
-        cp.wait_send()
-    for to, cp in ysends:
-        @pl.when(to != y)
-        def _():
-            cp.wait_send()
-    for ch in range(2):
-        own_copies(ch, sent)
-        for h in range(1, NZL):
-            relay(h, ch, sent, False)
 
 
 def step(tokens, queries, keys, targets, weights, m1, m2):
@@ -472,9 +501,10 @@
             V((XR, CA), F32), V((BR, CB), F32), V((XR, CA), BF), V((BR, CB), BF),
             V((NY - 1, YR, CA), BF), V((NX - 1, YR, CB), BF),
             V((NZH, YR, KVW), BF), V((ROWS, CA), BF), V((ROWS, CB), BF),
-            pltpu.SemaphoreType.DMA((6,)), pltpu.SemaphoreType.DMA((D // PW,)),
-            dma(6), dma(12), dma(21), dma(7), dma(21), dma(26),
-            dma(3), dma(8), dma(7), dma(3), dma(2), dma(7), dma(3), dma(3), dma(7),
+            V((XS, KVW), F32), V((YS, KVW), F32), V((XS, KVW), BF), V((YS, KVW), BF),
+            pltpu.SemaphoreType.DMA((6,)), pltpu.SemaphoreType.DMA((2,)), pltpu.SemaphoreType.DMA((D // PW,)),
+            dma(6), dma(12), dma(3), dma(7), dma(3), dma(26),
+            dma(3), dma(1), dma(1), dma(1), dma(2), dma(1), dma(1), dma(1), dma(1),
         ],
         compiler_params=pltpu.CompilerParams(
             collective_id=0, has_side_effects=True, vmem_limit_bytes=58 << 20

time: 89.1 us -> 88.5 us (level)
  no operation moved by 1% of the time
where the time goes in v3:
time: 88.5 us; the launch traced here: 88.3 us
  Pallas kernels  84.9 us (96%)
  other arithmetic  2.68 us (3%)
    pallas_call x1, Pallas kernels, step(): pl.pallas_call(kernel, out_shape=jax.ShapeDtypeStruct((ROWS, KVW), BF), i...  84.9 us
    sub x1, other arithmetic, per_device(): value_weights - outer_rate * inner_rate * (mean_direction + momentum_keep...  2.68 us

profile of v3, /device:TPU:2, one launch (start us, length us, event | category | flops | bytes accessed | tf_op | source)
XLA Modules:
  0.0 88.3 jit_solution(1146158629240581696)
XLA Ops:
  0.6 0.0 copy-start
  0.6 0.0 copy-start.1
  0.7 84.9 %shard_map.95 = bf16[512,512]{1,0:T(8,128)(2,1)} custom-call(bf16[128,4096]{1,0:T(8,128)(2,1)} %tok_h.1, bf16[128,2048]{1,0:T(8,128)(2,1)} %q_h.1, bf16[128,512]{1,0:T(8,128)(2,1)} %k_h.1, bf16[128,2048]{1,0:T(8,128)(2,1)} %t_h.1, f32[512,512]{1,0:T(8,128)} %w_h.1, f32[512,512]{1,0:T(8,128)} %bitcast.2, f32[512,512]{1,0:T(8,128)} %bitcast.3), custom_call_target="tpu_custom_call" | custom-call | tf_op jit(solution)/shard_map/pallas_call | solution.py:489
  85.6 0.0 copy-done
  85.6 0.0 copy-done.1
  85.6 2.7 %multiply_subtract_fusion = (f32[512,512]{1,0:T(8,128)}, f32[512,512]{1,0:T(8,128)}) fusion(f32[512,512]{1,0:T(8,128)S(1)} %copy-done, bf16[512,512]{1,0:T(8,128)(2,1)} %shard_map.95, f32[512,512]{1,0:T(8,128)S(1)} %copy-done.1), kind=kLoop, calls=%fused_computation | loop fusion | flops 2359296 | bytes 4718592 | tf_op jit(solution)/shard_map/sub | solution.py:523
Async XLA Ops:
  0.6 85.0 %copy-start = (f32[512,512]{1,0:T(8,128)S(1)}, f32[512,512]{1,0:T(8,128)}, u32[]{:S(2)}) copy-start(f32[512,512]{1,0:T(8,128)} %w_h.1) | copy-start | bytes 3145732
  0.6 85.0 %copy-start.1 = (f32[512,512]{1,0:T(8,128)S(1)}, f32[512,512]{1,0:T(8,128)}, u32[]{:S(2)}) copy-start(f32[512,512]{1,0:T(8,128)} %param.13) | copy-start | bytes 3145732

commit v4 on v3

--- a/solution.py
+++ b/solution.py
@@ -230,10 +230,15 @@
 
     rest = wall.at[0, pl.ds(0, (NY - 1) * YS)]
 
+    def hand(s, n, d):
+        piece = wa(s, at_x(d))
+        remote(piece, piece, wd, 1 + n, sibling).start()
+
     for n, s in enumerate(slots):
         got(wa(s, x), wz, 2 * n)
         go(wa(s, x), wx, n, x_r)
         go(wa(s, x), wx, 3 + n, x_l)
+        hand(s, n, 0)
         got(wb(s, y), wz, 2 * n + 1)
         piece = wb(s, y)
         many([(piece, piece, dev(y_=at_y(d))) for d in far_y], rest, wy, n)
@@ -247,8 +252,10 @@
     for n, s in enumerate(slots):
         got(wa(s, at_x(-1)), wx, n)
         go(wa(s, at_x(-1), 0), wx, 6 + n, x_r)
+        hand(s, n, -1)
         got(wa(s, at_x(1)), wx, 3 + n)
         go(wa(s, at_x(1), 1), wx, 9 + n, x_l)
+        hand(s, n, 1)
     acc[...] = term(f, 0) + term(f, 1)
     scores_of(2)
     scores_of(3)
@@ -264,7 +271,8 @@
     for n, s in enumerate(slots):
         got(wa(s, at_x(2), 0), wx, 6 + n)
         got(wa(s, at_x(2), 1), wx, 9 + n)
-        go(part(s, 0), wd, 1 + n, sibling)
+        hand(s, n, 2)
+        sends.append(remote(part(s, 0), part(s, 0), wd, 1 + n, sibling))
         acc[...] += term(s, 0) + term(s, 1)
     for n, s in enumerate(slots):
         o = s + 1 - 2 * c

time: 88.5 us -> 89 us (level)
  no operation moved by 1% of the time
where the time goes in v4:
time: 89 us; the launch traced here: 88.9 us
  Pallas kernels  85.5 us (96%)
  other arithmetic  2.68 us (3%)
    pallas_call x1, Pallas kernels, step(): pl.pallas_call(kernel, out_shape=jax.ShapeDtypeStruct((ROWS, KVW), BF), i...  85.5 us
    sub x1, other arithmetic, per_device(): value_weights - outer_rate * inner_rate * (mean_direction + momentum_keep...  2.68 us

profile of v4, /device:TPU:2, one launch (start us, length us, event | category | flops | bytes accessed | tf_op | source)
XLA Modules:
  0.0 88.9 jit_solution(18390542694153409163)
XLA Ops:
  0.6 0.0 copy-start
  0.6 0.0 copy-start.1
  0.7 85.5 %shard_map.95 = bf16[512,512]{1,0:T(8,128)(2,1)} custom-call(bf16[128,4096]{1,0:T(8,128)(2,1)} %tok_h.1, bf16[128,2048]{1,0:T(8,128)(2,1)} %q_h.1, bf16[128,512]{1,0:T(8,128)(2,1)} %k_h.1, bf16[128,2048]{1,0:T(8,128)(2,1)} %t_h.1, f32[512,512]{1,0:T(8,128)} %w_h.1, f32[512,512]{1,0:T(8,128)} %bitcast.2, f32[512,512]{1,0:T(8,128)} %bitcast.3), custom_call_target="tpu_custom_call" | custom-call | tf_op jit(solution)/shard_map/pallas_call | solution.py:497
  86.2 0.0 copy-done
  86.2 0.0 copy-done.1
  86.2 2.7 %multiply_subtract_fusion = (f32[512,512]{1,0:T(8,128)}, f32[512,512]{1,0:T(8,128)}) fusion(f32[512,512]{1,0:T(8,128)S(1)} %copy-done, bf16[512,512]{1,0:T(8,128)(2,1)} %shard_map.95, f32[512,512]{1,0:T(8,128)S(1)} %copy-done.1), kind=kLoop, calls=%fused_computation | loop fusion | flops 2359296 | bytes 4718592 | tf_op jit(solution)/shard_map/sub | solution.py:531
Async XLA Ops:
  0.6 85.5 %copy-start = (f32[512,512]{1,0:T(8,128)S(1)}, f32[512,512]{1,0:T(8,128)}, u32[]{:S(2)}) copy-start(f32[512,512]{1,0:T(8,128)} %w_h.1) | copy-start | bytes 3145732
  0.6 85.5 %copy-start.1 = (f32[512,512]{1,0:T(8,128)S(1)}, f32[512,512]{1,0:T(8,128)}, u32[]{:S(2)}) copy-start(f32[512,512]{1,0:T(8,128)} %param.13) | copy-start | bytes 3145732
